TPU v7x, 32 devices: a whole 2x2x4 slice. The times are simulated.
32 devices in a mesh: dp: 8 (over z, x), tensor: 4 (over y, core).
Axes of the slice: x: 2, y: 2, z: 4, core: 2. Of those that a mesh axis runs over, the one named last changes fastest.
Arguments:
- grads: bfloat16 [8, 2, 48, 256, 1024], P('dp', None, None, None, 'tensor'), may hold values from -70 to 70
- owner: int32 [48], replicated, may hold values from 0 to 7, as said below
- master: float32 [96, 256, 1024], P('dp', None, 'tensor'), may hold values from -0.1875 to 0.1875
- moment1: float32 [96, 256, 1024], P('dp', None, 'tensor'), may hold values from -2 to 2
- moment2: float32 [96, 256, 1024], P('dp', None, 'tensor'), may hold values from 0.01 to 1
Outputs:
- master_new: float32 [96, 256, 1024], P('dp', None, 'tensor')
- moment1_new: float32 [96, 256, 1024], P('dp', None, 'tensor')
- moment2_new: float32 [96, 256, 1024], P('dp', None, 'tensor')
- weights: bfloat16 [48, 256, 1024], P(None, None, 'tensor')
- norm_ratio: float32 [], replicated
Inputs may be any that keep to these rules, and one draw needn't show every extreme that they name: `owner`: no data index owns more than 12 groups, one owns exactly 12, and the first and the last index own at least one.
All inputs are finite; a program needn't handle non-finite values.
Results may differ from a plain program's by a relative error of at most 0.005.
Values may be sent and summed in bfloat16 or wider, within the bound.
A program may use at most 192 MiB of HBM per device.

v0:
```python
import math

import jax
import jax.numpy as jnp
from jax import lax
from jax.sharding import PartitionSpec as P

D = 1024
ROWS = 256
GROUPS = 48


beta_one = 0.9
beta_two = 0.98
learn_rate = 0.004
weight_decay = 0.01
adam_eps = 1e-06
step_count = 100


def order_within(owner):
    count = owner.shape[0]
    same = owner[:, None] == owner[None, :]
    earlier = (
        jnp.arange(count, dtype=jnp.int32)[:, None] > jnp.arange(count, dtype=jnp.int32)[None, :]
    )
    return jnp.sum((same & earlier).astype(jnp.int32), axis=1)


def adam_update(grad, master, moment1, moment2, clip):
    clipped = clip * grad
    first = beta_one * moment1 + (1.0 - beta_one) * clipped
    second = beta_two * moment2 + (1.0 - beta_two) * clipped * clipped
    fix_one = 1.0 - beta_one**step_count
    fix_two = 1.0 - beta_two**step_count
    update = first / fix_one / (jnp.sqrt(second / fix_two) + adam_eps) + weight_decay * master
    return (master - learn_rate * update, first, second)


def on_device(grads, owner, master, moment1, moment2):
    slot_count = master.shape[0]
    owners_all = lax.axis_size("dp")
    slots_all = owners_all * slot_count
    group_count = owner.shape[0]
    summed = grads[0, 0].astype(jnp.float32) + grads[0, 1].astype(jnp.float32)
    order_in = order_within(owner)
    slot_pos = owner * slot_count + order_in
    matches = slot_pos[None, :] == jnp.arange(slots_all, dtype=jnp.int32)[:, None]
    group_ids = jnp.sum(
        matches.astype(jnp.int32) * jnp.arange(group_count, dtype=jnp.int32)[None, :], axis=1
    )
    used = jnp.any(matches, axis=1).astype(jnp.float32)
    own_grad = lax.psum_scatter(
        (jnp.take(summed, group_ids, axis=0) * used[:, None, None]).astype(jnp.bfloat16),
        "dp",
        scatter_dimension=0,
        tiled=True,
    ).astype(jnp.float32)
    total = lax.psum(jnp.sum(own_grad * own_grad), ("dp", "tensor"))
    bound = math.sqrt(GROUPS * ROWS * D)
    norm_value = jnp.sqrt(total)
    norm_ratio = norm_value / bound
    clip = bound / jnp.maximum(norm_value, bound)
    master_new, moment1_new, moment2_new = adam_update(own_grad, master, moment1, moment2, clip)
    fresh = master_new.astype(jnp.bfloat16)
    every_slot = lax.all_gather(fresh, "dp", axis=0, tiled=True)
    weights = jnp.take(every_slot, slot_pos, axis=0)
    return (master_new, moment1_new, moment2_new, weights, norm_ratio)


def solution(mesh):
    return jax.shard_map(
        on_device,
        mesh=mesh,
        in_specs=(
            P("dp", None, None, None, "tensor"),
            P(),
            P("dp", None, "tensor"),
            P("dp", None, "tensor"),
            P("dp", None, "tensor"),
        ),
        out_specs=(
            P("dp", None, "tensor"),
            P("dp", None, "tensor"),
            P("dp", None, "tensor"),
            P(None, None, "tensor"),
            P(),
        ),
        check_vma=False,
    )
```

profile of v0, /device:TPU:0, one launch (start us, length us, event | category | flops | bytes accessed | tf_op | source)
XLA Modules:
  0.0 511.6 jit_solution(13863382293772455227)
XLA Ops:
  7.2 0.0 reduce-scatter.2.cloned.1.call-start
  7.2 0.9 convert_reduce_fusion
  8.1 0.7 compare_and_fusion
  8.8 0.1 select_reduce_fusion
  8.9 0.1 fusion.4
  9.0 11.7 %add_bitcast_fusion = f32[48,256,256]{2,1,0:T(8,128)} fusion(bf16[1,2,48,256,256]{4,3,2,1,0:T(8,128)(2,1)} %param.5), kind=kLoop, calls=%fused_computation.3 | loop fusion | flops 9437184 | bytes 25165824 | tf_op jit(solution)/shard_map/add | solution.py:45
  20.7 15.8 %gather_fusion = f32[96,256,256]{2,1,0:T(8,128)} fusion(f32[48,256,256]{2,1,0:T(8,128)} %add_bitcast_fusion, s32[1024]{0:T(1024)S(1)} %pad_clamp_fusion.1), kind=kCustom, calls=%fused_computation | custom fusion | bytes 50332032 | tf_op jit(solution)/shard_map/jit(_take)/gather | solution.py:54
  36.5 14.4 %multiply_convert_fusion = bf16[96,256,256]{2,1,0:T(8,128)(2,1)} fusion(f32[96,256,256]{2,1,0:T(8,128)} %gather_fusion, f32[96]{0:T(128)S(1)} %convert_element_type.31, pred[96]{0:T(512)(128)(4,1)S(1)} %compare_and_fusion.1), kind=kLoop, calls=%fused_computation.2 | loop fusion | flops 18874368 | bytes 37749216 | tf_op jit(solution)/shard_map/convert_element_type | solution.py:54
  50.9 0.0 copy-start
  50.9 0.0 reduce-scatter.2.cloned.1.call-update
  51.0 0.0 all-gather.2.cloned.1.call-start
  51.0 210.1 %reduce-scatter.2.cloned.1.call-done = bf16[12,256,256]{2,1,0:T(8,128)(2,1)} async-done(((bf16[96,256,256]{2,1,0:T(8,128)(2,1)}), bf16[12,256,256]{2,1,0:T(8,128)(2,1)}) %reduce-scatter.2.cloned.1.call-update) | async-done | bytes 1572880 | tf_op jit(solution)/shard_map/reduce_scatter | solution.py:53
  261.1 2.8 fusion.2
  263.9 39.6 %psum.7 = f32[]{:T(128)} all-reduce(f32[]{:T(128)} %fusion.2), channel_id=1, replica_groups=mesh['dp'=8,'tensor'=4] {'dp','tensor'}, use_global_device_ids=true, to_apply=%region_5.6 | all-reduce | flops 1 | bytes 8 | tf_op jit(solution)/shard_map/psum | solution.py:59
  304.2 0.0 copy-done
  304.2 7.0 %fusion.7 = (bf16[12,256,256]{2,1,0:T(8,128)(2,1)}, f32[12,256,256]{2,1,0:T(8,128)}, f32[12,256,256]{2,1,0:T(8,128)}, f32[12,256,256]{2,1,0:T(8,128)}) fusion(f32[12,256,256]{2,1,0:T(8,128)S(1)} %copy-done, bf16[12,256,256]{2,1,0:T(8,128)(2,1)} %reduce-scatter.2.cloned.1.call-done, f32[]{:T(128)S(6)} %div.21, f32[12,256,256]{2,1,0:T(8,128)} %param.8, ...), kind=kLoop, calls=%fused_computation.28 | loop fusion | flops 14155776 | bytes 22020100 | tf_op jit(solution)/shard_map/convert_element_type | solution.py:65
  311.3 0.0 all-gather.2.cloned.1.call-update
  311.3 176.5 %all-gather.2.cloned.1.call-done = bf16[96,256,256]{2,1,0:T(8,128)(2,1)} async-done(((bf16[12,256,256]{2,1,0:T(8,128)(2,1)}), bf16[96,256,256]{2,1,0:T(8,128)(2,1)}) %all-gather.2.cloned.1.call-update) | async-done | bytes 12582928 | tf_op jit(solution)/shard_map/all_gather | solution.py:66
  487.9 9.6 %gather_fusion.1 = bf16[48,256,256]{2,1,0:T(8,128)(2,1)} fusion(bf16[96,256,256]{2,1,0:T(8,128)(2,1)} %all-gather.2.cloned.1.call-done, s32[1024]{0:T(1024)S(1)} %pad_clamp_fusion), kind=kCustom, calls=%fused_computation.1 | custom fusion | bytes 12583104 | tf_op jit(solution)/shard_map/jit(_take)/gather | solution.py:67
  497.5 6.2 %broadcast_select_fusion = bf16[48,256,256]{2,1,0:T(8,128)(2,1)} fusion(bf16[48,256,256]{2,1,0:T(8,128)(2,1)} %gather_fusion.1, pred[48]{0:T(512)(128)(4,1)S(1)} %get-tuple-element.5), kind=kLoop, calls=%fused_computation.4 | loop fusion | flops 3145728 | bytes 12582960 | tf_op jit(solution)/shard_map/jit(_take)/select_n | solution.py:67
  (6 shorter events, 0.0 us)
Async XLA Ops:
  7.2 254.0 %reduce-scatter.2.cloned.1.call-start = ((), (), s32[]{:S(2)}) async-start(), calls=%async_computation.1 | async-start | bytes 14155776 | tf_op jit(solution)/shard_map/reduce_scatter | solution.py:53
  50.9 253.3 %copy-start = (f32[12,256,256]{2,1,0:T(8,128)S(1)}, f32[12,256,256]{2,1,0:T(8,128)}, u32[]{:S(2)}) copy-start(f32[12,256,256]{2,1,0:T(8,128)} %param.7) | copy-start | bytes 9437188
  51.0 436.9 %all-gather.2.cloned.1.call-start = ((), (), s32[]{:S(2)}) async-start(), calls=%async_computation.2 | async-start | bytes 14155776 | tf_op jit(solution)/shard_map/all_gather | solution.py:66
Sparse Core Ops, SparseCore 0:
  51.1 209.9 reduce-scatter.1
  311.4 176.4 all-gather.1
where the time goes:
time: 512 us
  waiting for transfers between devices  387 us (76%)
  other arithmetic  43.9 us (9%)
  blocking collectives  39.6 us (8%)
  local copies, waits for them, and re-layouts  25.4 us (5%)
  between operations  15.9 us (3%)
    reduce_scatter x1, waiting for transfers between devices, on_device(): lax.psum_scatter((jnp.take(summed, group_ids, axis=0) * used[:, None, Non...  210 us
    all_gather x1, waiting for transfers between devices, on_device(): every_slot = lax.all_gather(fresh, 'dp', axis=0, tiled=True)  177 us
    psum x1, blocking collectives, on_device(): total = lax.psum(jnp.sum(own_grad * own_grad), ('dp', 'tensor'))  39.6 us
    gather x1, local copies, waits for them, and re-layouts, on_device(): jnp.take(summed, group_ids, axis=0) * used[:, None, None]  15.8 us
    convert_element_type x1, other arithmetic, on_device(): (jnp.take(summed, group_ids, axis=0) * used[:, None, None]).astype(jnp.bf...  14.4 us
    add x1, other arithmetic, on_device(): summed = grads[0, 0].astype(jnp.float32) + grads[0, 1].astype(jnp.float32)  11.7 us
  transfers between devices with their start and end apart: 2, of which 2 were waited for; matrix products, arithmetic and copies ran while one was open for 0% of the time, Pallas kernels for 0%

commit v1 on v0

--- a/solution.py
+++ b/solution.py
@@ -1,8 +1,11 @@
+import functools
 import math
 
 import jax
 import jax.numpy as jnp
 from jax import lax
+from jax.experimental import pallas as pl
+from jax.experimental.pallas import tpu as pltpu
 from jax.sharding import PartitionSpec as P
 
 D = 1024
@@ -35,6 +38,352 @@
     fix_two = 1.0 - beta_two**step_count
     update = first / fix_one / (jnp.sqrt(second / fix_two) + adam_eps) + weight_decay * master
     return (master - learn_rate * update, first, second)
+
+
+Z = 4
+X = 2
+MESH = pl.DeviceIdType.MESH
+F32 = jnp.float32
+BF16 = jnp.bfloat16
+
+
+def place():
+    me = lax.axis_index("dp")
+    return lax.div(me, X), lax.rem(me, X), lax.axis_index("tensor")
+
+
+def barrier(z, x, tensor, lanes):
+    sem = pltpu.get_barrier_semaphore()
+    pl.semaphore_signal(sem, inc=1, device_id={"dp": z * X + 1 - x}, device_id_type=MESH)
+    for step in range(1, Z):
+        other = lax.rem(z + step, Z)
+        pl.semaphore_signal(sem, inc=1, device_id={"dp": other * X + x}, device_id_type=MESH)
+    if lanes > 1:
+        for step in range(1, lanes):
+            other = lax.rem(tensor + step, lanes)
+            pl.semaphore_signal(sem, inc=1, device_id={"tensor": other}, device_id_type=MESH)
+    pl.semaphore_wait(sem, Z + lanes - 1)
+
+
+def reduce_kernel(
+    n, lanes, ids_ref, used_ref, grads_ref, out_ref, total_ref,
+    held, xsend, xrecv, acc, rrecv, lrecv, norm1, norm2, norm3,
+    hsem, xs, xr, rs, rr, ls, lr, ns, nr,
+):
+    z, x, tensor = place()
+    rows = acc.shape[2]
+    part = 64
+    load = pltpu.make_async_copy(grads_ref, held, hsem)
+    load.start()
+    barrier(z, x, tensor, lanes)
+    load.wait()
+
+    def x_copy(k):
+        return pltpu.make_async_remote_copy(
+            src_ref=xsend.at[k], dst_ref=xrecv.at[k], send_sem=xs.at[k], recv_sem=xr.at[k],
+            device_id={"dp": z * X + 1 - x}, device_id_type=MESH)
+
+    def right_copy(k, d):
+        return pltpu.make_async_remote_copy(
+            src_ref=acc.at[k, d], dst_ref=rrecv.at[k, d], send_sem=rs.at[k, d], recv_sem=rr.at[k, d],
+            device_id={"dp": lax.rem(z + 1, Z) * X + x}, device_id_type=MESH)
+
+    def left_copy(k, d):
+        return pltpu.make_async_remote_copy(
+            src_ref=acc.at[k, d], dst_ref=lrecv.at[k, d], send_sem=ls.at[k, d], recv_sem=lr.at[k, d],
+            device_id={"dp": lax.rem(z + Z - 1, Z) * X + x}, device_id_type=MESH)
+
+    def local(k, col, d, span):
+        i = (k * X + col) * Z + d
+        g = ids_ref[i]
+        return (held[0, g, span].astype(F32) + held[1, g, span].astype(F32)) * used_ref[i]
+
+    def build(k):
+        for d in range(Z):
+            def body(j, c, d=d):
+                span = pl.ds(pl.multiple_of(j * part, part), part)
+                xsend[k, d, span] = local(k, 1 - x, d, span).astype(BF16)
+                return c
+            lax.fori_loop(0, rows // part, body, 0)
+        x_copy(k).start()
+
+    ahead = min(3, n)
+    for k in range(ahead):
+        build(k)
+
+    def tick(t, carry):
+        @pl.when(t + ahead < n)
+        def _():
+            build(t + ahead)
+
+        @pl.when(t < n)
+        def _():
+            x_copy(t).wait_recv()
+            for d in range(Z):
+                def body(j, c, d=d):
+                    span = pl.ds(pl.multiple_of(j * part, part), part)
+                    acc[t, d, span] = (local(t, x, d, span) + xrecv[t, d, span].astype(F32)).astype(BF16)
+                    return c
+                lax.fori_loop(0, rows // part, body, 0)
+
+        def stage(k, first, last, recv, copy, beyond):
+            @pl.when((k >= 0) & (k < n))
+            def _():
+                for d in range(Z):
+                    @pl.when(beyond(d))
+                    def _(d=d):
+                        @pl.when(jnp.logical_not(first))
+                        def _():
+                            copy(k, d).wait_recv()
+                            def body(j, c):
+                                span = pl.ds(pl.multiple_of(j * part, part), part)
+                                acc[k, d, span] = (acc[k, d, span].astype(F32) + recv[k, d, span].astype(F32)).astype(BF16)
+                                return c
+                            lax.fori_loop(0, rows // part, body, 0)
+                        copy(k, d).start()
+
+        stage(t - z, z == 0, z == Z - 1, rrecv, right_copy, lambda d: d > z)
+        stage(t - (Z - 1 - z), z == Z - 1, z == 0, lrecv, left_copy, lambda d: d < z)
+
+        k = t - (Z - 1)
+        @pl.when(k >= 0)
+        def _():
+            def first(j, c):
+                span = pl.ds(pl.multiple_of(j * part, part), part)
+                out_ref[k, span] = acc[k, z, span].astype(F32)
+                return c
+            lax.fori_loop(0, rows // part, first, 0)
+            for edge, copy, recv in ((0, right_copy, rrecv), (Z - 1, left_copy, lrecv)):
+                @pl.when(z != edge)
+                def _(copy=copy, recv=recv):
+                    copy(k, z).wait_recv()
+                    def body(j, c):
+                        span = pl.ds(pl.multiple_of(j * part, part), part)
+                        out_ref[k, span] = out_ref[k, span] + recv[k, z, span].astype(F32)
+                        return c
+                    lax.fori_loop(0, rows // part, body, 0)
+
+        return carry
+
+    lax.fori_loop(0, n + Z - 1, tick, 0)
+
+    width = out_ref.shape[2]
+    def squares(j, c):
+        k, j = lax.div(j, rows // part), lax.rem(j, rows // part)
+        v = out_ref[k, pl.ds(pl.multiple_of(j * part, part), part)]
+        v = jnp.sum((v * v).reshape(part // 8, 8, width), axis=0)
+        for m in range(width // 128):
+            c = c + v[:, m * 128:(m + 1) * 128]
+        return c
+    own = lax.fori_loop(0, n * (rows // part), squares, jnp.zeros((8, 128), F32))
+
+    def share(buf, mine, count, base, target):
+        def copy(slot, step, device):
+            return pltpu.make_async_remote_copy(
+                src_ref=buf.at[mine], dst_ref=buf.at[slot], send_sem=ns.at[base + step],
+                recv_sem=nr.at[base + step], device_id=device, device_id_type=MESH)
+        for step in range(1, count):
+            copy(mine, step, target(step)).start()
+        for step in range(1, count):
+            came = lax.rem(mine + count - step, count)
+            copy(came, step, target(step)).wait()
+        value = buf[0]
+        for i in range(1, count):
+            value = value + buf[i]
+        return value
+
+    norm1[x] = own
+    value = share(norm1, x, X, 0, lambda s: {"dp": z * X + lax.rem(x + s, X)})
+    norm2[z] = value
+    value = share(norm2, z, Z, X, lambda s: {"dp": lax.rem(z + s, Z) * X + x})
+    norm3[tensor] = value
+    value = share(norm3, tensor, lanes, X + Z, lambda s: {"tensor": lax.rem(tensor + s, lanes)})
+    total_ref[...] = value
+
+    def finish(k, carry):
+        x_copy(k).wait_send()
+        for d in range(Z):
+            @pl.when(d > z)
+            def _(d=d):
+                right_copy(k, d).wait_send()
+            @pl.when(d < z)
+            def _(d=d):
+                left_copy(k, d).wait_send()
+        return carry
+
+    lax.fori_loop(0, n, finish, 0)
+
+
+def reduce_slots(n, lanes, number, ids, used, grads):
+    _, groups, rows, width = grads.shape
+    block = (rows, width)
+    return pl.pallas_call(
+        functools.partial(reduce_kernel, n, lanes),
+        out_shape=(
+            jax.ShapeDtypeStruct((n,) + block, F32),
+            jax.ShapeDtypeStruct((8, 128), F32),
+        ),
+        in_specs=[
+            pl.BlockSpec(memory_space=pltpu.SMEM),
+            pl.BlockSpec(memory_space=pltpu.SMEM),
+            pl.BlockSpec(memory_space=pl.ANY),
+        ],
+        out_specs=(pl.BlockSpec(memory_space=pltpu.VMEM), pl.BlockSpec(memory_space=pltpu.VMEM)),
+        scratch_shapes=[
+            pltpu.VMEM((2, groups) + block, BF16),
+            pltpu.VMEM((n, Z) + block, BF16),
+            pltpu.VMEM((n, Z) + block, BF16),
+            pltpu.VMEM((n, Z) + block, BF16),
+            pltpu.VMEM((n, Z) + block, BF16),
+            pltpu.VMEM((n, Z) + block, BF16),
+            pltpu.VMEM((X, 8, 128), F32),
+            pltpu.VMEM((Z, 8, 128), F32),
+            pltpu.VMEM((lanes, 8, 128), F32),
+            pltpu.SemaphoreType.DMA,
+            pltpu.SemaphoreType.DMA((n,)),
+            pltpu.SemaphoreType.DMA((n,)),
+            pltpu.SemaphoreType.DMA((n, Z)),
+            pltpu.SemaphoreType.DMA((n, Z)),
+            pltpu.SemaphoreType.DMA((n, Z)),
+            pltpu.SemaphoreType.DMA((n, Z)),
+            pltpu.SemaphoreType.DMA((X + Z + lanes,)),
+            pltpu.SemaphoreType.DMA((X + Z + lanes,)),
+        ],
+        compiler_params=pltpu.CompilerParams(
+            collective_id=number, has_side_effects=True, vmem_limit_bytes=60 * 2**20
+        ),
+    )(ids, used, grads)
+
+
+def gather_kernel(n, fresh_ref, out_ref, osem, xs, xr, rs, ls, zr):
+    z, x, tensor = place()
+    barrier(z, x, tensor, 1)
+
+    def x_copy(src, k, d, col):
+        return pltpu.make_async_remote_copy(
+            src_ref=src, dst_ref=out_ref.at[k, col, d], send_sem=xs.at[k, d], recv_sem=xr.at[k, d],
+            device_id={"dp": z * X + 1 - x}, device_id_type=MESH)
+
+    def line_copy(src, k, d, step, sems):
+        return pltpu.make_async_remote_copy(
+            src_ref=src, dst_ref=out_ref.at[k, x, d], send_sem=sems.at[k, d], recv_sem=zr.at[k, d],
+            device_id={"dp": lax.rem(z + Z + step, Z) * X + x}, device_id_type=MESH)
+
+    def own_copy(k):
+        return pltpu.make_async_copy(fresh_ref.at[k], out_ref.at[k, x, z], osem.at[k])
+
+    def tick(t, carry):
+        @pl.when(t < n)
+        def _():
+            @pl.when(z < Z - 1)
+            def _():
+                line_copy(fresh_ref.at[t], t, z, 1, rs).start()
+            @pl.when(z > 0)
+            def _():
+                line_copy(fresh_ref.at[t], t, z, -1, ls).start()
+            x_copy(fresh_ref.at[t], t, z, x).start()
+            own_copy(t).start()
+        for hop in range(1, Z):
+            k = t - hop
+            @pl.when((k >= 0) & (k < n))
+            def _(k=k, hop=hop):
+                for d, step, sems, here, more in (
+                    (z - hop, 1, rs, z - hop >= 0, z < Z - 1),
+                    (z + hop, -1, ls, z + hop < Z, z > 0),
+                ):
+                    @pl.when(here)
+                    def _(d=d, step=step, sems=sems, more=more):
+                        block = out_ref.at[k, x, d]
+                        line_copy(block, k, d, step, sems).wait_recv()
+                        @pl.when(more)
+                        def _():
+                            line_copy(block, k, d, step, sems).start()
+                        x_copy(block, k, d, x).start()
+        return carry
+
+    lax.fori_loop(0, n + Z - 1, tick, 0)
+
+    def finish(k, carry):
+        own_copy(k).wait()
+        for d in range(Z):
+            x_copy(out_ref.at[k, x, d], k, d, x).wait_send()
+            x_copy(out_ref.at[k, x, d], k, d, 1 - x).wait_recv()
+            @pl.when((d <= z) & (z < Z - 1))
+            def _(d=d):
+                line_copy(out_ref.at[k, x, d], k, d, 1, rs).wait_send()
+            @pl.when((d >= z) & (z > 0))
+            def _(d=d):
+                line_copy(out_ref.at[k, x, d], k, d, -1, ls).wait_send()
+        return carry
+
+    lax.fori_loop(0, n, finish, 0)
+
+
+def gather_slots(number, fresh):
+    n = fresh.shape[0]
+    return pl.pallas_call(
+        functools.partial(gather_kernel, n),
+        out_shape=jax.ShapeDtypeStruct((n, X, Z) + fresh.shape[1:], BF16),
+        in_specs=[pl.BlockSpec(memory_space=pl.ANY)],
+        out_specs=pl.BlockSpec(memory_space=pl.ANY),
+        scratch_shapes=[pltpu.SemaphoreType.DMA((n,))] + [pltpu.SemaphoreType.DMA((n, Z))] * 5,
+        compiler_params=pltpu.CompilerParams(collective_id=number, has_side_effects=True),
+    )(fresh)
+
+
+def pick_kernel(pos_ref, slots_ref, out_ref, sems):
+    count = out_ref.shape[0]
+
+    def copy(g):
+        return pltpu.make_async_copy(slots_ref.at[pos_ref[g]], out_ref.at[g], sems.at[g])
+
+    def start(g, c):
+        copy(g).start()
+        return c
+
+    def done(g, c):
+        copy(g).wait()
+        return c
+
+    lax.fori_loop(0, count, start, 0)
+    lax.fori_loop(0, count, done, 0)
+
+
+def pick(pos, slots):
+    count = pos.shape[0]
+    return pl.pallas_call(
+        pick_kernel,
+        out_shape=jax.ShapeDtypeStruct((count,) + slots.shape[1:], slots.dtype),
+        in_specs=[pl.BlockSpec(memory_space=pltpu.SMEM), pl.BlockSpec(memory_space=pl.ANY)],
+        out_specs=pl.BlockSpec(memory_space=pl.ANY),
+        scratch_shapes=[pltpu.SemaphoreType.DMA((count,))],
+    )(pos, slots)
+
+
+def lookup(pos, slots_all):
+    matches = pos[None, :] == jnp.arange(slots_all, dtype=jnp.int32)[:, None]
+    ids = jnp.sum(
+        matches.astype(jnp.int32) * jnp.arange(pos.shape[0], dtype=jnp.int32)[None, :], axis=1
+    )
+    return ids, jnp.any(matches, axis=1).astype(F32)
+
+
+def on_slice(lanes, grads, owner, master, moment1, moment2):
+    slots = master.shape[0]
+    col, line = lax.rem(owner, X), lax.div(owner, X)
+    order_in = order_within(owner)
+    pos = (order_in * X + col) * Z + line
+    ids, used = lookup(pos, slots * X * Z)
+    own_grad, sums = reduce_slots(slots, lanes, 0, ids, used, grads[0])
+    total = jnp.sum(sums)
+    bound = math.sqrt(GROUPS * ROWS * D)
+    norm_value = jnp.sqrt(total)
+    norm_ratio = norm_value / bound
+    clip = bound / jnp.maximum(norm_value, bound)
+    master_new, moment1_new, moment2_new = adam_update(own_grad, master, moment1, moment2, clip)
+    every = gather_slots(1, master_new.astype(BF16))
+    weights = pick(pos, every.reshape((slots * X * Z,) + master.shape[1:]))
+    return (master_new, moment1_new, moment2_new, weights, norm_ratio)
 
 
 def on_device(grads, owner, master, moment1, moment2):
@@ -69,8 +418,11 @@
 
 
 def solution(mesh):
+    body = on_device
+    if mesh.shape["dp"] == Z * X:
+        body = functools.partial(on_slice, mesh.shape["tensor"])
     return jax.shard_map(
-        on_device,
+        body,
         mesh=mesh,
         in_specs=(
             P("dp", None, None, None, "tensor"),

time: 512 us -> 524 us (1.023)
  Pallas kernels: 0 us -> 510 us
  waiting for transfers between devices: 387 us -> 0 us
  blocking collectives: 39.6 us -> 0 us
  other arithmetic: 43.9 us -> 11.4 us
  local copies, waits for them, and re-layouts: 25.4 us -> 0.01 us
  between operations: 15.9 us -> 2.54 us
    pallas_call x0 -> x3, Pallas kernels: none -> 510 us  [the longest x1 193 us: pick(): pl.pallas_call(pick_kernel, out_shape=jax.ShapeDtypeStruct((count,) + slo...]
    reduce_scatter x1 -> x0, waiting for transfers between devices: 210 us -> none  [on_device(): lax.psum_scatter((jnp.take(summed, group_ids, axis=0) * used[:, None, Non...]
    all_gather x1 -> x0, waiting for transfers between devices: 177 us -> none  [on_device(): every_slot = lax.all_gather(fresh, 'dp', axis=0, tiled=True)]
    psum x1 -> x0, blocking collectives: 39.6 us -> none  [on_device(): total = lax.psum(jnp.sum(own_grad * own_grad), ('dp', 'tensor'))]
    gather x2 -> x0, local copies, waits for them, and re-layouts: 25.4 us -> none  [the longest x1 15.8 us: on_device(): jnp.take(summed, group_ids, axis=0) * used[:, None, None]]
    convert_element_type x3 -> x2, other arithmetic: 21.4 us -> 7.79 us  [the longest x1 7.27 us: on_slice(): every = gather_slots(1, master_new.astype(BF16))]
    add x1, other arithmetic: 11.7 us -> 0.67 us  [on_slice(): pos = (order_in * X + col) * Z + line]
    select_n x3 -> x0, other arithmetic: 6.17 us -> none  [the longest x2 6.16 us: on_device(): weights = jnp.take(every_slot, slot_pos, axis=0)]
  transfers between devices with their start and end apart: 2 -> 0, of which waited for: 2 -> 0; matrix products, arithmetic and copies ran while one was open for 0% -> 0% of each run, Pallas kernels for 0% -> 0%
where the time goes in v1:
time: 524 us; the launch traced here: 523 us
  Pallas kernels  510 us (97%)
  other arithmetic  11.4 us (2%)
    pallas_call x1, Pallas kernels, pick(): pl.pallas_call(pick_kernel, out_shape=jax.ShapeDtypeStruct((count,) + slo...  193 us
    pallas_call x1, Pallas kernels, reduce_slots(): pl.pallas_call(functools.partial(reduce_kernel, n, lanes), out_shape=(jax...  177 us
    pallas_call x1, Pallas kernels, gather_slots(): pl.pallas_call(functools.partial(gather_kernel, n), out_shape=jax.ShapeDt...  140 us

profile of v1, /device:TPU:0, one launch (start us, length us, event | category | flops | bytes accessed | tf_op | source)
XLA Modules:
  0.0 523.5 jit_solution(431690627608550949)
XLA Ops:
  0.6 0.9 convert_reduce_fusion
  1.5 0.7 fusion.4.pos_ref
  2.2 0.0 copy-start.1
  2.2 0.1 fusion.1
  2.3 0.5 convert_element_type.11.used_ref
  2.8 0.6 select_reduce_fusion.ids_ref
  3.4 0.0 copy-start
  3.4 176.7 %shard_map.92 = (f32[12,256,256]{2,1,0:T(8,128)}, f32[8,128]{1,0:T(8,128)}) custom-call(s32[96]{0:T(128)} %select_reduce_fusion.ids_ref, f32[96]{0:T(128)} %convert_element_type.11.used_ref, bf16[2,48,256,256]{3,2,1,0:T(8,128)(2,1)} %bitcast.3), custom_call_target="tpu_custom_call" | custom-call | tf_op jit(solution)/shard_map/pallas_call | solution.py:220
  180.1 0.0 copy-done.1
  180.1 1.3 reduce_sum.29
  182.1 0.0 copy-done
  182.1 7.3 %fusion.5 = (bf16[12,256,256]{2,1,0:T(8,128)(2,1)}, f32[12,256,256]{2,1,0:T(8,128)}, f32[12,256,256]{2,1,0:T(8,128)}, f32[12,256,256]{2,1,0:T(8,128)}) fusion(f32[12,256,256]{2,1,0:T(8,128)S(1)} %copy-done, f32[12,256,256]{2,1,0:T(8,128)} %get-tuple-element.8, f32[]{:T(128)S(6)} %div.31, f32[12,256,256]{2,1,0:T(8,128)} %param.8, f32[12,256,256]{2,1,0:T(8,128)} %param.9), kind=kLoop, calls=%fused_computation.15 | loop fusion | flops 13369344 | bytes 23592964 | tf_op jit(solution)/shard_map/convert_element_type | solution.py:384
  189.4 140.2 %shard_map.93 = bf16[12,2,4,256,256]{4,3,2,1,0:T(8,128)(2,1)} custom-call(bf16[12,256,256]{2,1,0:T(8,128)(2,1)} %get-tuple-element.9.fresh_ref), custom_call_target="tpu_custom_call" | custom-call | tf_op jit(solution)/shard_map/pallas_call | solution.py:324
  329.6 192.8 %shard_map.94 = bf16[48,256,256]{2,1,0:T(8,128)(2,1)} custom-call(s32[48]{0:T(128)} %copy-done.1, bf16[96,256,256]{2,1,0:T(8,128)(2,1)} %bitcast.2), custom_call_target="tpu_custom_call" | custom-call | tf_op jit(solution)/shard_map/pallas_call | solution.py:354
Async XLA Ops:
  2.2 177.9 %copy-start.1 = (s32[48]{0:T(128)}, s32[48]{0:T(128)S(1)}, u32[]{:S(2)}) copy-start(s32[48]{0:T(128)S(1)} %fusion.4.pos_ref) | copy-start | bytes 580
  3.4 178.7 %copy-start = (f32[12,256,256]{2,1,0:T(8,128)S(1)}, f32[12,256,256]{2,1,0:T(8,128)}, u32[]{:S(2)}) copy-start(f32[12,256,256]{2,1,0:T(8,128)} %param.7) | copy-start | bytes 9437188

commit v2 on v0

--- a/solution.py
+++ b/solution.py
@@ -1,8 +1,11 @@
+import functools
 import math
 
 import jax
 import jax.numpy as jnp
 from jax import lax
+from jax.experimental import pallas as pl
+from jax.experimental.pallas import tpu as pltpu
 from jax.sharding import PartitionSpec as P
 
 D = 1024
@@ -35,6 +38,483 @@
     fix_two = 1.0 - beta_two**step_count
     update = first / fix_one / (jnp.sqrt(second / fix_two) + adam_eps) + weight_decay * master
     return (master - learn_rate * update, first, second)
+
+
+Z = 4
+X = 2
+MESH = pl.DeviceIdType.MESH
+F32 = jnp.float32
+BF16 = jnp.bfloat16
+
+
+def place():
+    me = lax.axis_index("dp")
+    return lax.div(me, X), lax.rem(me, X), lax.axis_index("tensor")
+
+
+def barrier(z, x, tensor, lanes):
+    sem = pltpu.get_barrier_semaphore()
+    pl.semaphore_signal(sem, inc=1, device_id={"dp": z * X + 1 - x}, device_id_type=MESH)
+    for step in range(1, Z):
+        other = lax.rem(z + step, Z)
+        pl.semaphore_signal(sem, inc=1, device_id={"dp": other * X + x}, device_id_type=MESH)
+    if lanes > 1:
+        for step in range(1, lanes):
+            other = lax.rem(tensor + step, lanes)
+            pl.semaphore_signal(sem, inc=1, device_id={"tensor": other}, device_id_type=MESH)
+    pl.semaphore_wait(sem, Z + lanes - 1)
+
+
+def spread(z, x, out, xs, xr, rs, ls, zr):
+    def x_copy(src, k, d, col):
+        at = col * Z + d
+        return pltpu.make_async_remote_copy(
+            src_ref=src, dst_ref=out.at[k, at], send_sem=xs.at[k, d], recv_sem=xr.at[k, d],
+            device_id={"dp": z * X + 1 - x}, device_id_type=MESH)
+
+    def line_copy(src, k, d, step, sems):
+        return pltpu.make_async_remote_copy(
+            src_ref=src, dst_ref=out.at[k, x * Z + d], send_sem=sems.at[k, d], recv_sem=zr.at[k, d],
+            device_id={"dp": lax.rem(z + Z + step, Z) * X + x}, device_id_type=MESH)
+
+    def begin(src, k):
+        @pl.when(z < Z - 1)
+        def _():
+            line_copy(src, k, z, 1, rs).start()
+        @pl.when(z > 0)
+        def _():
+            line_copy(src, k, z, -1, ls).start()
+        x_copy(src, k, z, x).start()
+
+    def forward(k, hop):
+        for d, step, sems, here, more in (
+            (z - hop, 1, rs, z - hop >= 0, z < Z - 1),
+            (z + hop, -1, ls, z + hop < Z, z > 0),
+        ):
+            @pl.when(here)
+            def _(d=d, step=step, sems=sems, more=more):
+                block = out.at[k, x * Z + d]
+                line_copy(block, k, d, step, sems).wait_recv()
+                @pl.when(more)
+                def _():
+                    line_copy(block, k, d, step, sems).start()
+                x_copy(block, k, d, x).start()
+
+    def arrived(k):
+        for d in range(Z):
+            x_copy(out.at[k, x * Z + d], k, d, 1 - x).wait_recv()
+
+    def sent(k):
+        for d in range(Z):
+            x_copy(out.at[k, x * Z + d], k, d, x).wait_send()
+            @pl.when((d <= z) & (z < Z - 1))
+            def _(d=d):
+                line_copy(out.at[k, x * Z + d], k, d, 1, rs).wait_send()
+            @pl.when((d >= z) & (z > 0))
+            def _(d=d):
+                line_copy(out.at[k, x * Z + d], k, d, -1, ls).wait_send()
+
+    return begin, forward, arrived, sent
+
+
+def rows_loop(rows, body, part=64):
+    def one(j, c):
+        body(pl.ds(pl.multiple_of(j * part, part), part))
+        return c
+    lax.fori_loop(0, rows // part, one, 0)
+
+
+def scatter(z, x, local, xsend, xrecv, acc, rrecv, lrecv, xs, xr, rs, rr, ls, lr):
+    rows = acc.shape[2]
+
+    def x_copy(k):
+        return pltpu.make_async_remote_copy(
+            src_ref=xsend.at[k], dst_ref=xrecv.at[k], send_sem=xs.at[k], recv_sem=xr.at[k],
+            device_id={"dp": z * X + 1 - x}, device_id_type=MESH)
+
+    def right_copy(k, d):
+        return pltpu.make_async_remote_copy(
+            src_ref=acc.at[k, d], dst_ref=rrecv.at[k, d], send_sem=rs.at[k, d], recv_sem=rr.at[k, d],
+            device_id={"dp": lax.rem(z + 1, Z) * X + x}, device_id_type=MESH)
+
+    def left_copy(k, d):
+        return pltpu.make_async_remote_copy(
+            src_ref=acc.at[k, d], dst_ref=lrecv.at[k, d], send_sem=ls.at[k, d], recv_sem=lr.at[k, d],
+            device_id={"dp": lax.rem(z + Z - 1, Z) * X + x}, device_id_type=MESH)
+
+    def build(k):
+        for d in range(Z):
+            def body(span, d=d):
+                xsend[k, d, span] = local(k, 1 - x, d, span).astype(BF16)
+            rows_loop(rows, body)
+        x_copy(k).start()
+
+    def pair(k):
+        x_copy(k).wait_recv()
+        for d in range(Z):
+            def body(span, d=d):
+                acc[k, d, span] = (local(k, x, d, span) + xrecv[k, d, span].astype(F32)).astype(BF16)
+            rows_loop(rows, body)
+
+    def stage(k, first, recv, copy, beyond, order):
+        for d in order:
+            @pl.when(beyond(d))
+            def _(d=d):
+                @pl.when(jnp.logical_not(first))
+                def _():
+                    copy(k, d).wait_recv()
+                    def body(span):
+                        acc[k, d, span] = (acc[k, d, span].astype(F32) + recv[k, d, span].astype(F32)).astype(BF16)
+                    rows_loop(rows, body)
+                copy(k, d).start()
+
+    def right(k):
+        stage(k, z == 0, rrecv, right_copy, lambda d: d > z, range(Z - 1, -1, -1))
+
+    def left(k):
+        stage(k, z == Z - 1, lrecv, left_copy, lambda d: d < z, range(Z))
+
+    def final(k, out, row):
+        def first(span):
+            out[row, span] = acc[k, z, span].astype(F32)
+        rows_loop(rows, first)
+        for edge, copy, recv in ((0, right_copy, rrecv), (Z - 1, left_copy, lrecv)):
+            @pl.when(z != edge)
+            def _(copy=copy, recv=recv):
+                copy(k, z).wait_recv()
+                def body(span):
+                    out[row, span] = out[row, span] + recv[k, z, span].astype(F32)
+                rows_loop(rows, body)
+
+    def sent(k):
+        x_copy(k).wait_send()
+        for d in range(Z):
+            @pl.when(d > z)
+            def _(d=d):
+                right_copy(k, d).wait_send()
+            @pl.when(d < z)
+            def _(d=d):
+                left_copy(k, d).wait_send()
+
+    return build, pair, right, left, final, sent
+
+
+def when_in(k, n, f):
+    @pl.when((k >= 0) & (k < n))
+    def _():
+        f(k)
+
+
+def reduce_kernel(n, lanes, extra, *refs):
+    if extra:
+        ids_ref, used_ref, eids_ref, eused_ref, grads_ref, out_ref, total_ref, shared, *refs = refs
+        esems, refs = refs[:5], refs[5:]
+    else:
+        ids_ref, used_ref, grads_ref, out_ref, total_ref, *refs = refs
+    held, norm1, norm2, norm3, hsem, ns, nr, *work = refs
+    z, x, tensor = place()
+    slots, rows, width = out_ref.shape
+    part = 64
+    load = pltpu.make_async_copy(grads_ref, held, hsem)
+    load.start()
+    barrier(z, x, tensor, lanes)
+    load.wait()
+
+    def local(k, col, d, span):
+        i = (k * X + col) * Z + d
+        g = ids_ref[i]
+        return (held[0, g, span].astype(F32) + held[1, g, span].astype(F32)) * used_ref[i]
+
+    build, pair, right, left, final, sent = scatter(z, x, local, *work)
+    if extra:
+        begin, forward, arrived, gone = spread(z, x, shared, *esems)
+
+    def row_of(k):
+        return lax.rem(k - extra + slots, slots)
+
+    ahead = min(3, n)
+    for k in range(ahead):
+        build(k)
+
+    def tick(t, carry):
+        when_in(t + ahead, n, build)
+        when_in(t, n, pair)
+        when_in(t - z, n, right)
+        when_in(t - (Z - 1 - z), n, left)
+        when_in(t - (Z - 1), n, lambda k: final(k, out_ref, row_of(k)))
+        if extra:
+            @pl.when(t == Z - 1)
+            def _():
+                def body(span):
+                    shared[0, x * Z + z, span] = out_ref[slots - 1, span].astype(BF16)
+                rows_loop(rows, body)
+                begin(shared.at[0, x * Z + z], 0)
+            for hop in range(1, Z):
+                @pl.when(t == Z - 1 + 2 * hop)
+                def _(hop=hop):
+                    forward(0, hop)
+        return carry
+
+    lax.fori_loop(0, n + Z - 1, tick, 0)
+
+    def squares(j, c):
+        k, j = lax.div(j, rows // part), lax.rem(j, rows // part)
+        v = out_ref[row_of(k), pl.ds(pl.multiple_of(j * part, part), part)]
+        v = jnp.sum((v * v).reshape(part // 8, 8, width), axis=0)
+        for m in range(width // 128):
+            c = c + v[:, m * 128:(m + 1) * 128]
+        return c
+    own = lax.fori_loop(0, n * (rows // part), squares, jnp.zeros((8, 128), F32))
+
+    def share(buf, mine, count, base, target):
+        def copy(slot, step, device):
+            return pltpu.make_async_remote_copy(
+                src_ref=buf.at[mine], dst_ref=buf.at[slot], send_sem=ns.at[base + step],
+                recv_sem=nr.at[base + step], device_id=device, device_id_type=MESH)
+        for step in range(1, count):
+            copy(mine, step, target(step)).start()
+        for step in range(1, count):
+            came = lax.rem(mine + count - step, count)
+            copy(came, step, target(step)).wait()
+        value = buf[0]
+        for i in range(1, count):
+            value = value + buf[i]
+        return value
+
+    norm1[x] = own
+    value = share(norm1, x, X, 0, lambda s: {"dp": z * X + lax.rem(x + s, X)})
+    norm2[z] = value
+    value = share(norm2, z, Z, X, lambda s: {"dp": lax.rem(z + s, Z) * X + x})
+    norm3[tensor] = value
+    value = share(norm3, tensor, lanes, X + Z, lambda s: {"tensor": lax.rem(tensor + s, lanes)})
+    total_ref[...] = value
+
+    if extra:
+        arrived(0)
+        for s in range(n - 1, slots):
+            i = s - (n - 1)
+            def body(span, s=s, i=i):
+                out_ref[s, span] = shared[0, eids_ref[i], span].astype(F32) * eused_ref[i]
+            rows_loop(rows, body)
+        gone(0)
+
+    def finish(k, carry):
+        sent(k)
+        return carry
+
+    lax.fori_loop(0, n, finish, 0)
+
+
+def work_shapes(n, block):
+    return [pltpu.VMEM((n, Z) + block, BF16)] * 5 + [
+        pltpu.SemaphoreType.DMA((n,)),
+        pltpu.SemaphoreType.DMA((n,)),
+    ] + [pltpu.SemaphoreType.DMA((n, Z))] * 4
+
+
+def reduce_slots(n, slots, lanes, number, tables, grads):
+    _, groups, rows, width = grads.shape
+    block = (rows, width)
+    extra = 1 if n < slots else 0
+    more = []
+    if extra:
+        more = [pltpu.VMEM((1, X * Z) + block, BF16)] + [pltpu.SemaphoreType.DMA((1, Z))] * 5
+    return pl.pallas_call(
+        functools.partial(reduce_kernel, n, lanes, extra),
+        out_shape=(
+            jax.ShapeDtypeStruct((slots,) + block, F32),
+            jax.ShapeDtypeStruct((8, 128), F32),
+        ),
+        in_specs=[pl.BlockSpec(memory_space=pltpu.SMEM)] * len(tables)
+        + [pl.BlockSpec(memory_space=pl.ANY)],
+        out_specs=(pl.BlockSpec(memory_space=pltpu.VMEM), pl.BlockSpec(memory_space=pltpu.VMEM)),
+        scratch_shapes=more + [
+            pltpu.VMEM((2, groups) + block, BF16),
+            pltpu.VMEM((X, 8, 128), F32),
+            pltpu.VMEM((Z, 8, 128), F32),
+            pltpu.VMEM((lanes, 8, 128), F32),
+            pltpu.SemaphoreType.DMA,
+            pltpu.SemaphoreType.DMA((X + Z + lanes,)),
+            pltpu.SemaphoreType.DMA((X + Z + lanes,)),
+        ] + work_shapes(n, block),
+        compiler_params=pltpu.CompilerParams(
+            collective_id=number, has_side_effects=True, vmem_limit_bytes=60 * 2**20
+        ),
+    )(*tables, grads)
+
+
+def gather_kernel(n, extra, *refs):
+    if extra:
+        sids_ref, mine_ref, *refs = refs
+    fresh_ref, out_ref, osem, *refs = refs
+    esems, refs = refs[:5], refs[5:]
+    z, x, tensor = place()
+    slots, rows, width = fresh_ref.shape
+    plain = n - extra
+    barrier(z, x, tensor, 1)
+    begin, forward, arrived, gone = spread(z, x, out_ref, *esems)
+    if extra:
+        summed, mixed, *work = refs
+
+        def local(k, col, d, span):
+            i = col * Z + d
+            return fresh_ref[sids_ref[i], span].astype(F32) * mine_ref[i]
+
+        build, pair, right, left, final, sent = scatter(z, x, local, *work)
+        build(0)
+
+    def own_copy(src, k):
+        return pltpu.make_async_copy(src, out_ref.at[k, x * Z + z], osem.at[k])
+
+    def tick(t, carry):
+        @pl.when(t < plain)
+        def _():
+            begin(fresh_ref.at[t], t)
+            own_copy(fresh_ref.at[t], t).start()
+        if extra:
+            @pl.when(t == 1)
+            def _():
+                pair(0)
+            @pl.when(t == 1 + z)
+            def _():
+                right(0)
+            @pl.when(t == Z - z)
+            def _():
+                left(0)
+            @pl.when(t == Z + 1)
+            def _():
+                final(0, summed, 0)
+                def body(span):
+                    mixed[0, span] = summed[0, span].astype(BF16)
+                rows_loop(rows, body)
+            @pl.when(t == plain)
+            def _():
+                begin(mixed.at[0], plain)
+                own_copy(mixed.at[0], plain).start()
+        for hop in range(1, Z):
+            when_in(t - hop, n, lambda k, hop=hop: forward(k, hop))
+        return carry
+
+    lax.fori_loop(0, n + Z - 1, tick, 0)
+
+    def finish(k, carry):
+        own_copy(fresh_ref.at[0], k).wait()
+        arrived(k)
+        gone(k)
+        return carry
+
+    lax.fori_loop(0, n, finish, 0)
+    if extra:
+        sent(0)
+
+
+def gather_slots(n, number, tables, fresh):
+    slots, rows, width = fresh.shape
+    block = (rows, width)
+    extra = 1 if n < slots else 0
+    more = []
+    if extra:
+        more = [pltpu.VMEM((1,) + block, F32), pltpu.VMEM((1,) + block, BF16)] + work_shapes(1, block)
+    return pl.pallas_call(
+        functools.partial(gather_kernel, n, extra),
+        out_shape=jax.ShapeDtypeStruct((n, X * Z) + block, BF16),
+        in_specs=[pl.BlockSpec(memory_space=pltpu.SMEM)] * len(tables)
+        + [pl.BlockSpec(memory_space=pltpu.VMEM)],
+        out_specs=pl.BlockSpec(memory_space=pl.ANY),
+        scratch_shapes=[pltpu.SemaphoreType.DMA((n,))]
+        + [pltpu.SemaphoreType.DMA((n, Z))] * 5 + more,
+        compiler_params=pltpu.CompilerParams(
+            collective_id=number, has_side_effects=True, vmem_limit_bytes=32 * 2**20
+        ),
+    )(*tables, fresh)
+
+
+def pick_kernel(pos_ref, *refs):
+    out_ref = refs[-1]
+    for i, ref in enumerate(refs[:-1]):
+        out_ref[i] = ref[0]
+
+
+def pick(pos, slots):
+    count = pos.shape[0]
+    rows, width = slots.shape[1:]
+    wide = math.gcd(count, 8)
+    return pl.pallas_call(
+        pick_kernel,
+        out_shape=jax.ShapeDtypeStruct((count, rows, width), slots.dtype),
+        grid_spec=pltpu.PrefetchScalarGridSpec(
+            num_scalar_prefetch=1,
+            grid=(count // wide,),
+            in_specs=[
+                pl.BlockSpec((1, rows, width), lambda i, p, j=j: (p[i * wide + j], 0, 0))
+                for j in range(wide)
+            ],
+            out_specs=pl.BlockSpec((wide, rows, width), lambda i, p: (i, 0, 0)),
+        ),
+    )(pos, *([slots] * wide))
+
+
+def lookup(pos, slots_all):
+    matches = pos[None, :] == jnp.arange(slots_all, dtype=jnp.int32)[:, None]
+    ids = jnp.sum(
+        matches.astype(jnp.int32) * jnp.arange(pos.shape[0], dtype=jnp.int32)[None, :], axis=1
+    )
+    return ids, jnp.any(matches, axis=1).astype(F32)
+
+
+REGULAR = 7
+
+
+def on_slice(lanes, grads, owner, master, moment1, moment2):
+    slots = master.shape[0]
+    count = owner.shape[0]
+    own_count = X * Z
+    me = lax.axis_index("dp")
+    col, line = lax.rem(owner, X), lax.div(owner, X)
+    order_in = order_within(owner)
+    regular = (order_in * X + col) * Z + line
+
+    over = order_in >= REGULAR
+    before = jnp.arange(count)[None, :] < jnp.arange(count)[:, None]
+    shared = jnp.sum((over[None, :] & before).astype(jnp.int32), axis=1)
+    fits = jnp.sum(over.astype(jnp.int32)) <= own_count
+
+    def few_reduce(part):
+        pos = jnp.where(over, shared, own_count + regular)
+        ids, used = lookup(pos, (REGULAR + 1) * own_count)
+        wanted = jnp.arange(REGULAR, slots, dtype=jnp.int32)
+        hit = (owner[None, :] == me) & (order_in[None, :] == wanted[:, None])
+        eids = jnp.sum(hit.astype(jnp.int32) * jnp.minimum(shared, own_count - 1)[None, :], axis=1)
+        eused = jnp.any(hit, axis=1).astype(F32)
+        return reduce_slots(REGULAR + 1, slots, lanes, 0, (ids, used, eids, eused), part)
+
+    def all_reduce(part):
+        ids, used = lookup(regular, slots * own_count)
+        return reduce_slots(slots, slots, lanes, 1, (ids, used), part)
+
+    own_grad, sums = lax.cond(fits, few_reduce, all_reduce, grads[0])
+    total = jnp.sum(sums)
+    bound = math.sqrt(GROUPS * ROWS * D)
+    norm_value = jnp.sqrt(total)
+    norm_ratio = norm_value / bound
+    clip = bound / jnp.maximum(norm_value, bound)
+    master_new, moment1_new, moment2_new = adam_update(own_grad, master, moment1, moment2, clip)
+
+    def few_gather(fresh):
+        place_of = jnp.arange(own_count, dtype=jnp.int32)
+        hit = over[None, :] & (shared[None, :] == place_of[:, None]) & (owner[None, :] == me)
+        sids = jnp.sum(hit.astype(jnp.int32) * order_in[None, :], axis=1)
+        mine = jnp.any(hit, axis=1).astype(F32)
+        every = gather_slots(REGULAR + 1, 2, (sids, mine), fresh)
+        pos = jnp.where(over, REGULAR * own_count + jnp.minimum(shared, own_count - 1), regular)
+        return pick(pos, every.reshape((-1,) + fresh.shape[1:]))
+
+    def all_gather(fresh):
+        every = gather_slots(slots, 3, (), fresh)
+        return pick(regular, every.reshape((-1,) + fresh.shape[1:]))
+
+    weights = lax.cond(fits, few_gather, all_gather, master_new.astype(BF16))
+    return (master_new, moment1_new, moment2_new, weights, norm_ratio)
 
 
 def on_device(grads, owner, master, moment1, moment2):
@@ -69,8 +549,11 @@
 
 
 def solution(mesh):
+    body = on_device
+    if mesh.shape["dp"] == Z * X:
+        body = functools.partial(on_slice, mesh.shape["tensor"])
     return jax.shard_map(
-        on_device,
+        body,
         mesh=mesh,
         in_specs=(
             P("dp", None, None, None, "tensor"),

time: 512 us -> 268 us (0.52)
  waiting for transfers between devices: 387 us -> 0 us
  Pallas kernels: 0 us -> 247 us
  blocking collectives: 39.6 us -> 0 us
  other arithmetic: 43.9 us -> 13.9 us
  local copies, waits for them, and re-layouts: 25.4 us -> 3.23 us
  between operations: 15.9 us -> 3.2 us
    pallas_call x0 -> x3, Pallas kernels: none -> 247 us  [the longest x1 131 us: reduce_slots(): pl.pallas_call(functools.partial(reduce_kernel, n, lanes, extra), out_sha...]
    reduce_scatter x1 -> x0, waiting for transfers between devices: 210 us -> none  [on_device(): lax.psum_scatter((jnp.take(summed, group_ids, axis=0) * used[:, None, Non...]
    all_gather x1 -> x0, waiting for transfers between devices: 177 us -> none  [on_device(): every_slot = lax.all_gather(fresh, 'dp', axis=0, tiled=True)]
    psum x1 -> x0, blocking collectives: 39.6 us -> none  [on_device(): total = lax.psum(jnp.sum(own_grad * own_grad), ('dp', 'tensor'))]
    gather x2 -> x0, local copies, waits for them, and re-layouts: 25.4 us -> none  [the longest x1 15.8 us: on_device(): jnp.take(summed, group_ids, axis=0) * used[:, None, None]]
    convert_element_type x3 -> x4, other arithmetic: 21.4 us -> 7.88 us  [the longest x1 6.84 us: on_slice(): weights = lax.cond(fits, few_gather, all_gather, master_new.astype(BF16))]
    add x1 -> x2, other arithmetic: 11.7 us -> 1.31 us  [the longest x1 1.3 us: on_slice(): regular = (order_in * X + col) * Z + line]
    select_n x3 -> x1, other arithmetic: 6.17 us -> 0.49 us  [few_gather(): jnp.where(over, REGULAR * own_count + jnp.minimum(shared, own_count - 1),...]
  transfers between devices with their start and end apart: 2 -> 0, of which waited for: 2 -> 0; matrix products, arithmetic and copies ran while one was open for 0% -> 0% of each run, Pallas kernels for 0% -> 0%
where the time goes in v2:
time: 268 us
  Pallas kernels  247 us (92%)
  other arithmetic  13.9 us (5%)
  local copies, waits for them, and re-layouts  3.23 us (1%)
  between operations  3.2 us (1%)
    pallas_call x1, Pallas kernels, reduce_slots(): pl.pallas_call(functools.partial(reduce_kernel, n, lanes, extra), out_sha...  131 us
    pallas_call x1, Pallas kernels, gather_slots(): pl.pallas_call(functools.partial(gather_kernel, n, extra), out_shape=jax....  108 us
    pallas_call x1, Pallas kernels, pick(): pl.pallas_call(pick_kernel, out_shape=jax.ShapeDtypeStruct((count, rows,...  7.51 us
    convert_element_type x1, other arithmetic, on_slice(): weights = lax.cond(fits, few_gather, all_gather, master_new.astype(BF16))  6.84 us

profile of v2, /device:TPU:0, one launch (start us, length us, event | category | flops | bytes accessed | tf_op | source)
XLA Modules:
  0.0 267.6 jit_solution(15401074631735151297)
XLA Ops:
  0.6 0.9 convert_reduce_fusion.1
  1.6 0.1 convert_reduce_fusion
  1.7 1.3 fusion.10
  3.6 0.0 copy-start.2
  3.6 134.7 %conditional.2 = ((f32[12,256,256]{2,1,0:T(8,128)}, f32[8,128]{1,0:T(8,128)S(1)})) conditional(s32[]{:T(128)} %convert_element_type.34, (s32[48]{0:T(128)S(1)}, bf16[2,48,256,256]{3,2,1,0:T(8,128)(2,1)}) %tuple.36, (s32[48]{0:T(128)S(1)}, pred[48]{0:T(512)(128)(4,1)S(1)}, s32[48]{0:T(128)S(1)}, s32[]{:T(128)}, s32[48]{0:T(128)}, ...), branch_computations={%region_3.0_spmd, %region_6.11_spmd} | conditional | flops 22944 | bytes 2874 | solution.py:495
  3.7 0.8 broadcast_compare_fusion
  4.5 0.7 select_reduce_fusion.2.refs_2_
  5.2 0.2 fusion.2
  5.4 0.5 convert_element_type.11.refs_3_
  5.9 0.1 fusion.1
  6.0 0.6 select_reduce_fusion.1.refs_0_
  6.6 0.5 convert_element_type.10.refs_1_
  7.1 131.2 %branch_1_fun.3 = (f32[12,256,256]{2,1,0:T(8,128)}, f32[8,128]{1,0:T(8,128)S(1)}) custom-call(s32[64]{0:T(128)} %select_reduce_fusion.1.refs_0_, f32[64]{0:T(128)} %convert_element_type.10.refs_1_, s32[5]{0:T(128)} %select_reduce_fusion.2.refs_2_, f32[5]{0:T(128)} %convert_element_type.11.refs_3_, bf16[2,48,256,256]{3,2,1,0:T(8,128)(2,1)} %get-tuple-element.47.refs_4_), custom_call_target="tpu_custom_call" | custom-call | tf_op jit(solution)/shard_map/cond/branch_1_fun/pallas_call | solution.py:322
  138.3 0.6 reduce_sum.75
  139.7 0.0 copy-done.2
  139.7 0.0 copy-start.3
  139.7 6.8 %fusion.11 = (bf16[12,256,256]{2,1,0:T(8,128)(2,1)S(1)}, f32[12,256,256]{2,1,0:T(8,128)}, f32[12,256,256]{2,1,0:T(8,128)}, f32[12,256,256]{2,1,0:T(8,128)}) fusion(f32[12,256,256]{2,1,0:T(8,128)S(1)} %copy-done.2, f32[12,256,256]{2,1,0:T(8,128)} %get-tuple-element.65, f32[]{:T(128)S(6)} %div.31, f32[12,256,256]{2,1,0:T(8,128)} %param.12, ...), kind=kLoop, calls=%fused_computation.37 | loop fusion | flops 13369344 | bytes 23592964 | tf_op jit(solution)/shard_map/convert_element_type | solution.py:516
  146.5 0.0 copy-done.3
  146.5 120.0 %conditional.3 = (bf16[48,256,256]{2,1,0:T(8,128)(2,1)}) conditional(s32[]{:T(128)} %convert_element_type.34, (bf16[12,256,256]{2,1,0:T(8,128)(2,1)S(1)}, s32[48]{0:T(128)S(1)}) %tuple.22, (s32[48]{0:T(128)S(1)}, pred[48]{0:T(512)(128)(4,1)S(1)}, s32[48]{0:T(128)S(1)}, s32[]{:T(128)}, s32[48]{0:T(128)S(1)}, /*index=5*/s32[48]{0:T(128)S(1)}, ...), branch_computations={%region_12.13_spmd, %region_13.16_spmd} | conditional | flops 3640 | bytes 50331684 | solution.py:516
  146.5 0.5 add_select_fusion.1.pos_ref
  147.0 0.1 select_reduce_fusion.3.refs_0_
  147.1 0.1 fusion.5
  147.3 108.5 %branch_1_fun.4 = bf16[8,8,256,256]{3,2,1,0:T(8,128)(2,1)S(1)} custom-call(s32[8]{0:T(128)S(1)} %select_reduce_fusion.3.refs_0_, f32[8]{0:T(128)S(1)} %convert_element_type.18.refs_1_, bf16[12,256,256]{2,1,0:T(8,128)(2,1)S(1)} %get-tuple-element.56.refs_2_), custom_call_target="tpu_custom_call" | custom-call | tf_op jit(solution)/shard_map/cond/branch_1_fun/pallas_call | solution.py:418
  255.8 0.0 copy-start.1
  255.8 3.2 %copy-done.1 = bf16[8,8,256,256]{3,2,1,0:T(8,128)(2,1)} copy-done((bf16[8,8,256,256]{3,2,1,0:T(8,128)(2,1)}, bf16[8,8,256,256]{3,2,1,0:T(8,128)(2,1)S(1)}, u32[]{:S(2)}) %copy-start.1) | copy-done | bytes 8388632 | tf_op jit(solution)/shard_map/cond
  259.0 7.5 %branch_1_fun.5 = bf16[48,256,256]{2,1,0:T(8,128)(2,1)} custom-call(s32[48]{0:T(128)} %add_select_fusion.1.pos_ref, bf16[64,256,256]{2,1,0:T(8,128)(2,1)} %bitcast.11, bf16[64,256,256]{2,1,0:T(8,128)(2,1)} %bitcast.12, bf16[64,256,256]{2,1,0:T(8,128)(2,1)} %bitcast.13, bf16[64,256,256]{2,1,0:T(8,128)(2,1)} %bitcast.14, bf16[64,256,256]{2,1,0:T(8,128)(2,1)} %bitcast.15, ...), custom_call_target="tpu_custom_call" | custom-call | tf_op jit(solution)/shard_map/cond/branch_1_fun/pallas_call | solution.py:442
  (5 shorter events, 0.0 us)
Async XLA Ops:
  3.6 136.0 %copy-start.2 = (f32[12,256,256]{2,1,0:T(8,128)S(1)}, f32[12,256,256]{2,1,0:T(8,128)}, u32[]{:S(2)}) copy-start(f32[12,256,256]{2,1,0:T(8,128)} %param.11) | copy-start | bytes 9437188
  139.7 6.9 %copy-start.3 = (s32[48]{0:T(128)S(1)}, s32[48]{0:T(128)}, u32[]{:S(2)}) copy-start(s32[48]{0:T(128)} %param.10) | copy-start | bytes 580
  255.8 3.2 %copy-start.1 = (bf16[8,8,256,256]{3,2,1,0:T(8,128)(2,1)}, bf16[8,8,256,256]{3,2,1,0:T(8,128)(2,1)S(1)}, u32[]{:S(2)}) copy-start(bf16[8,8,256,256]{3,2,1,0:T(8,128)(2,1)S(1)} %branch_1_fun.4) | copy-start | bytes 25165828 | tf_op jit(solution)/shard_map/cond
